TPU v7x, 32 devices: a whole 2x2x4 slice. The times are simulated.
32 devices in a mesh: groups: 1, tm: 32 (over z, y, x, core).
Axes of the slice: x: 2, y: 2, z: 4, core: 2. Of those that a mesh axis runs over, the one named last changes fastest.
Arguments:
- latents: bfloat16 [32, 512, 512], P(('groups', 'tm')), may hold values from -21 to 21
- w_query: bfloat16 [512, 512], replicated, may hold values from -3 to 3
- w_key: bfloat16 [512, 512], replicated, may hold values from -3 to 3
- w_value: bfloat16 [512, 512], replicated, may hold values from -0.25 to 0.25
- w_out: bfloat16 [512, 512], replicated, may hold values from -0.25 to 0.25
- w_time: bfloat16 [3, 512, 512], replicated, may hold values from -0.15625 to 0.15625
- w_space: bfloat16 [3, 3, 512, 512], replicated, may hold values from -0.09375 to 0.09375
- tile_starts: int32 [4], P('groups'), may hold values from 0 to 25, as said below
Outputs:
- decoded: bfloat16 [32, 512, 512], P(('groups', 'tm'))
Inputs may be any that keep to these rules, and one draw needn't show every extreme that they name: `tile_starts`: Increasing; the first is 0, the last is (3) * 8 + 1, and every other start t lies within 2 frames of t * 8.
All inputs are finite; a program needn't handle non-finite values.
Results may differ from a plain program's by a relative error of at most 0.0096.
Values may be sent and summed in bfloat16 or wider, within the bound.
A program may use at most 64 MiB of HBM per device.

v0:
```python
import jax
import jax.numpy as jnp
from jax import lax
from jax.sharding import PartitionSpec as P

PH = 16
PW = 32
OV = 2
epsilon = 1e-06


def passed_along(block, axis, distance):
    devices = range(lax.axis_size(axis))
    route = [(i - distance, i) for i in devices if i - distance in devices]
    return lax.ppermute(block, axis, route)


def rms_norm(array):
    wide = array.astype(jnp.float32)
    return (wide * lax.rsqrt(jnp.mean(wide * wide, axis=-1, keepdims=True) + epsilon)).astype(
        jnp.bfloat16
    )


def project(array, weight):
    extent = array.shape
    product = jnp.dot(array.reshape(-1, extent[-1]), weight, preferred_element_type=jnp.float32)
    return product.reshape(extent[:-1] + (weight.shape[-1],))


def tile_frames(frames, starts):
    reached = starts[None, :] <= frames[:, None]
    new_start = jnp.max(jnp.where(reached, starts[None, :], 0), axis=1)
    earlier = starts[None, :] < new_start[:, None]
    old_start = jnp.max(jnp.where(earlier, starts[None, :], 0), axis=1)
    inside = frames - new_start
    shared = jnp.logical_and(new_start > 0, inside < OV)
    fade = jnp.where(shared, (inside + 1).astype(jnp.float32) / float(OV + 1), jnp.float32(1.0))
    return (new_start, old_start, fade[:, None, None])


def attend(triple):
    queries, key_rows, values = triple
    length = queries.shape[0]
    scale = queries.shape[-1] ** (-0.5)
    scores = (
        jnp.einsum("fipc,gipc->ipfg", queries, key_rows, preferred_element_type=jnp.float32) * scale
    )
    order = jnp.arange(length)
    causal = order[:, None] >= order[None, :]
    scores = jnp.where(causal[None, None], scores, jnp.float32(-1e30))
    peak = jnp.max(scores, axis=-1, keepdims=True)
    expo = jnp.exp(scores - peak)
    weights = (expo / jnp.sum(expo, axis=-1, keepdims=True)).astype(jnp.bfloat16)
    return jnp.einsum(
        "ipfg,gipc->fipc", weights, values, preferred_element_type=jnp.float32
    ).astype(jnp.bfloat16)


def time_blend(padded, frames, starts, w_time):
    length = frames.shape[0]
    extent = padded.shape
    channels = extent[-1]
    flattened = padded.reshape(-1, channels)
    products = [
        jnp.dot(flattened, w_time[lag_index], preferred_element_type=jnp.float32).reshape(
            extent[0], -1, channels
        )
        for lag_index in range(3)
    ]
    new_start, old_start, fade = tile_frames(frames, starts)

    def mixed(context):
        summed = jnp.zeros((length,) + products[0].shape[1:], jnp.float32)
        for lag_index in range(3):
            actual = jnp.minimum(lag_index, frames - context)
            for delta_back in range(lag_index + 1):
                chosen = (actual == delta_back).astype(jnp.float32)[:, None, None]
                summed = (
                    summed + chosen * products[lag_index][2 - delta_back : 2 - delta_back + length]
                )
        return summed

    blended = fade * jax.nn.silu(mixed(new_start)) + (1.0 - fade) * jax.nn.silu(mixed(old_start))
    return blended.astype(jnp.bfloat16)


def space_mix(blended, hidden, w_space):
    length = blended.shape[0]
    channels = blended.shape[-1]
    spatial = blended.reshape(length, PH, PW, channels)
    padded = jnp.pad(spatial, ((0, 0), (1, 1), (1, 1), (0, 0)))
    summed = hidden.reshape(-1, channels).astype(jnp.float32)
    for row_shift in range(3):
        for col_shift in range(3):
            window = padded[:, row_shift : row_shift + PH, col_shift : col_shift + PW].reshape(
                -1, channels
            )
            summed = summed + jnp.dot(
                window, w_space[row_shift, col_shift], preferred_element_type=jnp.float32
            )
    return summed.reshape(length, PH * PW, channels).astype(jnp.bfloat16)


def body(latents, w_query, w_key, w_value, w_out, w_time, w_space, tile_starts):
    frames_dev, row_count, channels = latents.shape
    devices_tm = lax.axis_size("tm")
    share = row_count // devices_tm
    normed = rms_norm(latents).reshape(frames_dev, devices_tm, share, channels)
    queries = project(normed, w_query).astype(jnp.bfloat16)
    key_rows = project(normed, w_key).astype(jnp.bfloat16)
    values = project(normed, w_value).astype(jnp.bfloat16)
    attended = attend(
        (
            lax.all_to_all(queries, "tm", split_axis=1, concat_axis=0, tiled=True),
            lax.all_to_all(key_rows, "tm", split_axis=1, concat_axis=0, tiled=True),
            lax.all_to_all(values, "tm", split_axis=1, concat_axis=0, tiled=True),
        )
    )
    attended = lax.all_to_all(attended, "tm", split_axis=0, concat_axis=1, tiled=True).reshape(
        frames_dev, row_count, channels
    )
    hidden = (latents.astype(jnp.float32) + project(attended, w_out)).astype(jnp.bfloat16)
    smooth = rms_norm(hidden)
    reach = (frames_dev + 1) // frames_dev
    pieces = [passed_along(smooth, "tm", stride) for stride in range(reach, 0, -1)]
    earlier = jnp.concatenate(pieces, axis=0)
    offset = lax.axis_index("tm") * frames_dev
    frames = offset + jnp.arange(frames_dev)
    blended = time_blend(jnp.concatenate([earlier, smooth], axis=0), frames, tile_starts, w_time)
    return space_mix(blended, hidden, w_space)


def solution(mesh):
    placed = (P(("groups", "tm"), None, None), P(), P(), P(), P(), P(), P(), P("groups"))
    return jax.shard_map(
        body, mesh=mesh, in_specs=placed, out_specs=P(("groups", "tm"), None, None), check_vma=False
    )
```

profile of v0, /device:TPU:9, one launch (start us, length us, event | category | flops | bytes accessed | tf_op | source)
XLA Modules:
  0.0 117.2 jit_solution(4229719521326724587)
XLA Ops:
  0.0 1.3 %fusion.11 = f32[512]{0:T(512)S(1)} fusion(bf16[1,512,512]{2,1,0:T(8,128)(2,1)} %param.8), kind=kLoop, calls=%fused_computation.33 | loop fusion | flops 785920 | bytes 526336 | tf_op jit(solution)/shard_map/reduce_sum | solution.py:20
  1.3 1.3 %fusion.12 = bf16[1,512,512]{2,1,0:T(8,128)(2,1)S(1)} fusion(bf16[1,512,512]{2,1,0:T(8,128)(2,1)} %param.8, f32[512]{0:T(512)S(1)} %add_rsqrt_fusion.1), kind=kLoop, calls=%fused_computation.34 | loop fusion | flops 786432 | bytes 1050624 | tf_op jit(solution)/shard_map/convert_element_type | solution.py:20
  2.6 2.3 %fusion.7 = bf16[1,32,16,512]{3,2,0,1:T(8,128)(2,1)} fusion(bf16[32,16,512]{2,1,0:T(8,128)(2,1)S(1)} %bitcast.117, bf16[512,512]{1,0:T(8,128)(2,1)} %param.10), kind=kOutput, calls=%fused_computation.28 | convolution fusion | flops 268697600 | bytes 1572864 | tf_op jit(solution)/shard_map/dot_general | solution.py:27
  4.9 6.4 %all-to-all-start.2 = ((bf16[1,32,16,512]{3,2,0,1:T(8,128)(2,1)}), bf16[1,32,16,512]{3,2,0,1:T(8,128)(2,1)S(1)}, u32[]{:S(2)}, u32[]{:S(2)}) async-start(bf16[1,32,16,512]{3,2,0,1:T(8,128)(2,1)} %fusion.7), calls=%async_computation.2 | async-start | bytes 1048576 | tf_op jit(solution)/shard_map/all_to_all | solution.py:116
  11.3 1.2 %fusion.6 = bf16[1,32,16,512]{3,2,0,1:T(8,128)(2,1)} fusion(bf16[32,16,512]{2,1,0:T(8,128)(2,1)S(1)} %bitcast.118, bf16[512,512]{1,0:T(8,128)(2,1)S(1)} %copy-done.3), kind=kOutput, calls=%fused_computation.27 | convolution fusion | flops 268697600 | bytes 1572864 | tf_op jit(solution)/shard_map/dot_general | solution.py:27
  12.5 13.0 %all-to-all-done.2 = bf16[1,32,16,512]{3,2,0,1:T(8,128)(2,1)S(1)} async-done(((bf16[1,32,16,512]{3,2,0,1:T(8,128)(2,1)}), bf16[1,32,16,512]{3,2,0,1:T(8,128)(2,1)S(1)}, u32[]{:S(2)}, u32[]{:S(2)}) %all-to-all-start.2) | async-done | bytes 524320 | tf_op jit(solution)/shard_map/all_to_all | solution.py:116
  25.5 4.4 %all-to-all-start.1 = ((bf16[1,32,16,512]{3,2,0,1:T(8,128)(2,1)}), bf16[1,32,16,512]{3,2,0,1:T(8,128)(2,1)S(1)}, u32[]{:S(2)}, u32[]{:S(2)}) async-start(bf16[1,32,16,512]{3,2,0,1:T(8,128)(2,1)} %fusion.6), calls=%async_computation.1 | async-start | bytes 1048576 | tf_op jit(solution)/shard_map/all_to_all | solution.py:115
  29.9 1.2 %fusion.5 = bf16[1,32,16,512]{3,2,0,1:T(8,128)(2,1)} fusion(bf16[32,16,512]{2,1,0:T(8,128)(2,1)S(1)} %bitcast.119, bf16[512,512]{1,0:T(8,128)(2,1)S(1)} %copy-done.4), kind=kOutput, calls=%fused_computation.26 | convolution fusion | flops 268697600 | bytes 1572864 | tf_op jit(solution)/shard_map/dot_general | solution.py:27
  31.1 13.0 %all-to-all-done.1 = bf16[1,32,16,512]{3,2,0,1:T(8,128)(2,1)S(1)} async-done(((bf16[1,32,16,512]{3,2,0,1:T(8,128)(2,1)}), bf16[1,32,16,512]{3,2,0,1:T(8,128)(2,1)S(1)}, u32[]{:S(2)}, u32[]{:S(2)}) %all-to-all-start.1) | async-done | bytes 524320 | tf_op jit(solution)/shard_map/all_to_all | solution.py:115
  44.1 4.4 %all-to-all-start = ((bf16[1,32,16,512]{3,2,0,1:T(8,128)(2,1)}), bf16[1,32,16,512]{3,2,0,1:T(8,128)(2,1)S(1)}, u32[]{:S(2)}, u32[]{:S(2)}) async-start(bf16[1,32,16,512]{3,2,0,1:T(8,128)(2,1)} %fusion.5), calls=%async_computation | async-start | bytes 1048576 | tf_op jit(solution)/shard_map/all_to_all | solution.py:117
  48.5 0.7 fusion.57
  49.2 13.5 %all-to-all-done = bf16[1,32,16,512]{3,2,0,1:T(8,128)(2,1)S(1)} async-done(((bf16[1,32,16,512]{3,2,0,1:T(8,128)(2,1)}), bf16[1,32,16,512]{3,2,0,1:T(8,128)(2,1)S(1)}, u32[]{:S(2)}, u32[]{:S(2)}) %all-to-all-start) | async-done | bytes 524320 | tf_op jit(solution)/shard_map/all_to_all | solution.py:117
  62.7 0.5 fusion.4
  63.5 18.4 %all_to_all.16 = bf16[32,1,16,512]{3,2,1,0:T(8,128)(2,1)S(1)} all-to-all(bf16[32,1,16,512]{3,2,1,0:T(8,128)(2,1)S(1)} %copy.25), channel_id=1, replica_groups=mesh['groups'=1,'tm'=32] {'tm'}, dimensions={0} | all-to-all | bytes 1048576 | tf_op jit(solution)/shard_map/all_to_all | solution.py:120
  82.0 0.5 fusion.13
  82.7 3.0 %collective-permute-start.1 = (bf16[1,512,512]{2,1,0:T(8,128)(2,1)S(1)}, bf16[1,512,512]{2,1,0:T(8,128)(2,1)}, u32[]{:S(2)}, u32[]{:S(2)}) collective-permute-start(bf16[1,512,512]{2,1,0:T(8,128)(2,1)S(1)} %fusion.14), channel_id=1, source_target_pairs={{0,1},{1,2},{2,3},{3,4},{4,5},{5,6},{6,7},{7,8},{8,9},{9,10},{10,1... | collective-permute-start | bytes 1572872 | tf_op jit(solution)/shard_map/ppermute | solution.py:15
  85.7 3.6 %collective-permute-start = (bf16[1,512,512]{2,1,0:T(8,128)(2,1)S(1)}, bf16[1,512,512]{2,1,0:T(8,128)(2,1)}, u32[]{:S(2)}, u32[]{:S(2)}) collective-permute-start(bf16[1,512,512]{2,1,0:T(8,128)(2,1)S(1)} %fusion.14), channel_id=1, source_target_pairs={{0,2},{1,3},{2,4},{3,5},{4,6},{5,7},{6,8},{7,9},{8,10},{9,11},{10,... | collective-permute-start | bytes 1572872 | tf_op jit(solution)/shard_map/ppermute | solution.py:15
  89.3 0.6 fusion.55
  89.9 1.2 %fusion.56 = s32[]{:T(128)} fusion(s32[4]{0:T(128)S(1)} %copy-done.5, s32[]{:T(128)} %fusion.55), kind=kLoop, calls=%fused_computation.91 | loop fusion | flops 11 | bytes 24 | tf_op jit(solution)/shard_map/reduce_max | solution.py:35
  93.1 1.3 %collective-permute-done.1 = bf16[1,512,512]{2,1,0:T(8,128)(2,1)} collective-permute-done((bf16[1,512,512]{2,1,0:T(8,128)(2,1)S(1)}, bf16[1,512,512]{2,1,0:T(8,128)(2,1)}, u32[]{:S(2)}, u32[]{:S(2)}) %collective-permute-start.1) | collective-permute-done | bytes 524320 | tf_op jit(solution)/shard_map/ppermute | solution.py:15
  94.4 12.5 %collective-permute-done = bf16[1,512,512]{2,1,0:T(8,128)(2,1)} collective-permute-done((bf16[1,512,512]{2,1,0:T(8,128)(2,1)S(1)}, bf16[1,512,512]{2,1,0:T(8,128)(2,1)}, u32[]{:S(2)}, u32[]{:S(2)}) %collective-permute-start) | collective-permute-done | bytes 524320 | tf_op jit(solution)/shard_map/ppermute | solution.py:15
  106.9 1.4 %pad_maximum_fusion = bf16[3,512,512]{2,1,0:T(8,128)(2,1)S(1)} fusion(bf16[1,512,512]{2,1,0:T(8,128)(2,1)S(1)} %fusion.14, bf16[1,512,512]{2,1,0:T(8,128)(2,1)} %collective-permute-done.1, bf16[1,512,512]{2,1,0:T(8,128)(2,1)} %collective-permute-done), kind=kLoop, calls=%fused_computation.1 | loop fusion | flops 1572864 | bytes 3145728 | tf_op jit(solution)/shard_map/concatenate | solution.py:130
  108.2 1.0 fusion.28
  109.2 1.0 fusion.30
  110.2 1.5 %add_convert_fusion = bf16[512,512]{1,0:T(8,128)(2,1)S(1)} fusion(f32[1536,512]{1,0:T(8,128)S(1)} %fusion.28, f32[1536,512]{1,0:T(8,128)S(1)} %fusion.30, bf16[1536,512]{1,0:T(8,128)(2,1)S(1)} %bitcast.116, f32[]{:T(128)S(6)} %sub.31, f32[]{:T(128)S(6)} %select_n.22, f32[]{:T(128)S(6)} %convert_element_type.146, f32[]{:T(128)S(6)} %convert_element_type.145, ...), kind=kOutput, calls=%fused_computation.37 | convolution fusion | flops 277348352 | bytes 6815800 | tf_op jit(solution)/shard_map/dot_general | solution.py:66
  111.8 0.7 pad_slice_fusion
  112.5 0.4 convolution_add_fusion.8
  113.3 0.4 convolution_add_fusion.6
  114.2 0.4 convolution_add_fusion.4
  114.7 0.4 convolution_add_fusion.3
  115.6 0.4 convolution_add_fusion.1
  116.0 1.2 %fusion.3 = bf16[1,512,512]{2,1,0:T(8,128)(2,1)} fusion(f32[512,512]{1,0:T(8,128)S(1)} %convolution_add_fusion.1, bf16[512,512]{1,0:T(8,128)(2,1)S(1)} %bitcast.122, bf16[3,3,512,512]{3,2,1,0:T(8,128)(2,1)S(1)} %bitcast.121), kind=kOutput, calls=%fused_computation.24 | convolution fusion | flops 268959744 | bytes 2621440 | tf_op jit(solution)/shard_map/dot_general | solution.py:99
  (25 shorter events, 1.8 us)
Async XLA Ops:
  0.0 82.0 %copy-start = (bf16[512,512]{1,0:T(8,128)(2,1)S(1)}, bf16[512,512]{1,0:T(8,128)(2,1)}, u32[]{:S(2)}) copy-start(bf16[512,512]{1,0:T(8,128)(2,1)} %param.12) | copy-start | bytes 1572868
  0.0 11.2 %copy-start.3 = (bf16[512,512]{1,0:T(8,128)(2,1)S(1)}, bf16[512,512]{1,0:T(8,128)(2,1)}, u32[]{:S(2)}) copy-start(bf16[512,512]{1,0:T(8,128)(2,1)} %param.9) | copy-start | bytes 1572868
  1.3 28.6 %copy-start.4 = (bf16[512,512]{1,0:T(8,128)(2,1)S(1)}, bf16[512,512]{1,0:T(8,128)(2,1)}, u32[]{:S(2)}) copy-start(bf16[512,512]{1,0:T(8,128)(2,1)} %param.11) | copy-start | bytes 1572868
  4.9 20.6 %all-to-all-start.2 = ((bf16[1,32,16,512]{3,2,0,1:T(8,128)(2,1)}), bf16[1,32,16,512]{3,2,0,1:T(8,128)(2,1)S(1)}, u32[]{:S(2)}, u32[]{:S(2)}) async-start(bf16[1,32,16,512]{3,2,0,1:T(8,128)(2,1)} %fusion.7), calls=%async_computation.2 | async-start | bytes 1048576 | tf_op jit(solution)/shard_map/all_to_all | solution.py:116
  25.5 18.6 %all-to-all-start.1 = ((bf16[1,32,16,512]{3,2,0,1:T(8,128)(2,1)}), bf16[1,32,16,512]{3,2,0,1:T(8,128)(2,1)S(1)}, u32[]{:S(2)}, u32[]{:S(2)}) async-start(bf16[1,32,16,512]{3,2,0,1:T(8,128)(2,1)} %fusion.6), calls=%async_computation.1 | async-start | bytes 1048576 | tf_op jit(solution)/shard_map/all_to_all | solution.py:115
  31.1 50.9 %copy-start.1 = (bf16[1,512,512]{2,1,0:T(8,128)(2,1)S(1)}, bf16[1,512,512]{2,1,0:T(8,128)(2,1)}, u32[]{:S(2)}) copy-start(bf16[1,512,512]{2,1,0:T(8,128)(2,1)} %param.8) | copy-start | bytes 1572868
  44.1 18.6 %all-to-all-start = ((bf16[1,32,16,512]{3,2,0,1:T(8,128)(2,1)}), bf16[1,32,16,512]{3,2,0,1:T(8,128)(2,1)S(1)}, u32[]{:S(2)}, u32[]{:S(2)}) async-start(bf16[1,32,16,512]{3,2,0,1:T(8,128)(2,1)} %fusion.5), calls=%async_computation | async-start | bytes 1048576 | tf_op jit(solution)/shard_map/all_to_all | solution.py:117
  63.2 26.1 %copy-start.5 = (s32[4]{0:T(128)S(1)}, s32[4]{0:T(128)}, u32[]{:S(2)}) copy-start(s32[4]{0:T(128)} %param.15) | copy-start | bytes 52
  82.0 26.3 %copy-start.2 = (bf16[3,512,512]{2,1,0:T(8,128)(2,1)S(1)}, bf16[3,512,512]{2,1,0:T(8,128)(2,1)}, u32[]{:S(2)}) copy-start(bf16[3,512,512]{2,1,0:T(8,128)(2,1)} %param.13) | copy-start | bytes 4718596
  82.7 11.7 %collective-permute-start.1 = (bf16[1,512,512]{2,1,0:T(8,128)(2,1)S(1)}, bf16[1,512,512]{2,1,0:T(8,128)(2,1)}, u32[]{:S(2)}, u32[]{:S(2)}) collective-permute-start(bf16[1,512,512]{2,1,0:T(8,128)(2,1)S(1)} %fusion.14), channel_id=1, source_target_pairs={{0,1},{1,2},{2,3},{3,4},{4,5},{5,6},{6,7},{7,8},{8,9},{9,10},{10,1... | collective-permute-start | bytes 1572872 | tf_op jit(solution)/shard_map/ppermute | solution.py:15
  85.7 21.1 %collective-permute-start = (bf16[1,512,512]{2,1,0:T(8,128)(2,1)S(1)}, bf16[1,512,512]{2,1,0:T(8,128)(2,1)}, u32[]{:S(2)}, u32[]{:S(2)}) collective-permute-start(bf16[1,512,512]{2,1,0:T(8,128)(2,1)S(1)} %fusion.14), channel_id=1, source_target_pairs={{0,2},{1,3},{2,4},{3,5},{4,6},{5,7},{6,8},{7,9},{8,10},{9,11},{10,... | collective-permute-start | bytes 1572872 | tf_op jit(solution)/shard_map/ppermute | solution.py:15
  109.2 3.2 %slice-start = ((s8[4718592]{0:T(1024)(128)(4,1)}), s8[4194304]{0:T(1024)(128)(4,1)S(1)}, s32[]{:S(2)}) async-start(s8[4718592]{0:T(1024)(128)(4,1)} %bitcast.120), calls=%async_computation.4 | async-start | bytes 8388608
  110.2 2.2 %slice-start.1 = ((s8[4718592]{0:T(1024)(128)(4,1)}), s8[524288]{0:T(1024)(128)(4,1)S(1)}, s32[]{:S(2)}) async-start(s8[4718592]{0:T(1024)(128)(4,1)} %bitcast.120), calls=%async_computation.5 | async-start | bytes 1048576
where the time goes:
time: 118 us; the launch traced here: 117 us
  waiting for transfers between devices  53.1 us (45%)
  starting transfers between devices  21.8 us (18%)
  blocking collectives  18.4 us (16%)
  matrix products  14.7 us (12%)
  other arithmetic  6.02 us (5%)
  between operations  2.18 us (2%)
    all_to_all x1, blocking collectives, body(): lax.all_to_all(attended, 'tm', split_axis=0, concat_axis=1, tiled=True)  18.4 us
    ppermute x2, waiting for transfers between devices, passed_along(): return lax.ppermute(block, axis, route)  13.7 us
    all_to_all x1, waiting for transfers between devices, body(): lax.all_to_all(values, 'tm', split_axis=1, concat_axis=0, tiled=True)  13.5 us
    all_to_all x1, waiting for transfers between devices, body(): lax.all_to_all(key_rows, 'tm', split_axis=1, concat_axis=0, tiled=True)  13 us
    all_to_all x1, waiting for transfers between devices, body(): lax.all_to_all(queries, 'tm', split_axis=1, concat_axis=0, tiled=True)  13 us
    ppermute x2, starting transfers between devices, passed_along(): return lax.ppermute(block, axis, route)  6.57 us
    all_to_all x1, starting transfers between devices, body(): lax.all_to_all(key_rows, 'tm', split_axis=1, concat_axis=0, tiled=True)  6.36 us
    dot_general x4, matrix products, project(): jnp.dot(array.reshape(-1, extent[-1]), weight, preferred_element_type=jnp...  5.27 us
  transfers between devices with their start and end apart: 5, of which 5 were waited for; matrix products, arithmetic and copies ran while one was open for 4% of the time, Pallas kernels for 0%

commit v1 on v0

--- a/solution.py
+++ b/solution.py
@@ -112,7 +112,12 @@
     values = project(normed, w_value).astype(jnp.bfloat16)
     attended = attend(
         (
-            lax.all_to_all(queries, "tm", split_axis=1, concat_axis=0, tiled=True),
+            jnp.concatenate(
+                lax.all_to_all(
+                    jnp.stack(jnp.split(queries, lax.axis_size("tm"), axis=1)), "tm", 0, 0
+                ),
+                axis=0,
+            ),
             lax.all_to_all(key_rows, "tm", split_axis=1, concat_axis=0, tiled=True),
             lax.all_to_all(values, "tm", split_axis=1, concat_axis=0, tiled=True),
         )

time: 118 us -> 136 us (1.15)
  local copies, waits for them, and re-layouts: 0.99 us -> 20.4 us
    unnamed x16 -> x47, local copies, waits for them, and re-layouts: 0.04 us -> 18.8 us
    all_to_all x1, starting transfers between devices: 4.42 us -> 6.36 us  [body(): lax.all_to_all(jnp.stack(jnp.split(queries, lax.axis_size('tm'), axis=1))...]
    all_to_all x1, starting transfers between devices: 6.36 us -> 4.42 us  [body(): lax.all_to_all(key_rows, 'tm', split_axis=1, concat_axis=0, tiled=True)]
where the time goes in v1:
time: 136 us
  waiting for transfers between devices  53.1 us (39%)
  starting transfers between devices  21.8 us (16%)
  local copies, waits for them, and re-layouts  20.4 us (15%)
  blocking collectives  18.4 us (14%)
  matrix products  14 us (10%)
  other arithmetic  5.97 us (4%)
  between operations  2.21 us (2%)
    unnamed x47, local copies, waits for them, and re-layouts  18.8 us
    all_to_all x1, blocking collectives, body(): lax.all_to_all(attended, 'tm', split_axis=0, concat_axis=1, tiled=True)  18.4 us
    ppermute x2, waiting for transfers between devices, passed_along(): return lax.ppermute(block, axis, route)  13.7 us
    all_to_all x1, waiting for transfers between devices, body(): lax.all_to_all(values, 'tm', split_axis=1, concat_axis=0, tiled=True)  13.5 us
    all_to_all x1, waiting for transfers between devices, body(): lax.all_to_all(jnp.stack(jnp.split(queries, lax.axis_size('tm'), axis=1))...  13 us
    all_to_all x1, waiting for transfers between devices, body(): lax.all_to_all(key_rows, 'tm', split_axis=1, concat_axis=0, tiled=True)  13 us
    ppermute x2, starting transfers between devices, passed_along(): return lax.ppermute(block, axis, route)  6.57 us
    all_to_all x1, starting transfers between devices, body(): lax.all_to_all(jnp.stack(jnp.split(queries, lax.axis_size('tm'), axis=1))...  6.36 us
  transfers between devices with their start and end apart: 5, of which 5 were waited for; matrix products, arithmetic and copies ran while one was open for 4% of the time, Pallas kernels for 0%

profile of v1, /device:TPU:9, one launch (start us, length us, event | category | flops | bytes accessed | tf_op | source)
XLA Modules:
  0.0 135.9 jit_solution(15416567641050121901)
XLA Ops:
  0.0 1.3 fusion.11
  1.3 1.2 fusion.12
  2.5 1.5 %fusion.6 = bf16[1,32,16,512]{3,2,1,0:T(8,128)(2,1)S(1)} fusion(bf16[32,16,512]{2,1,0:T(8,128)(2,1)S(1)} %bitcast.239, bf16[512,512]{1,0:T(8,128)(2,1)} %param.9), kind=kOutput, calls=%fused_computation.27 | convolution fusion | flops 268697600 | bytes 1572864 | tf_op jit(solution)/shard_map/dot_general | solution.py:27
  4.1 0.6 constant_dynamic-update-slice_fusion.31
  5.9 0.6 constant_dynamic-update-slice_fusion.28
  6.5 0.6 constant_dynamic-update-slice_fusion.27
  7.1 0.6 constant_dynamic-update-slice_fusion.26
  7.7 0.6 constant_dynamic-update-slice_fusion.25
  8.3 0.6 constant_dynamic-update-slice_fusion.24
  8.9 0.6 constant_dynamic-update-slice_fusion.23
  23.5 6.4 %all-to-all-start.1 = ((bf16[32,1,1,16,512]{4,3,2,1,0:T(8,128)(2,1)}), bf16[32,1,1,16,512]{4,3,2,1,0:T(8,128)(2,1)S(1)}, u32[]{:S(2)}, u32[]{:S(2)}) async-start(bf16[32,1,1,16,512]{4,3,2,1,0:T(8,128)(2,1)} %constant_dynamic-update-slice_fusion), calls=%async_computation.1 | async-start | bytes 1048576 | tf_op jit(solution)/shard_map/all_to_all | solution.py:116
  29.9 1.2 fusion.7
  31.1 13.0 %all-to-all-done.1 = bf16[32,1,1,16,512]{4,3,2,1,0:T(8,128)(2,1)S(1)} async-done(((bf16[32,1,1,16,512]{4,3,2,1,0:T(8,128)(2,1)}), bf16[32,1,1,16,512]{4,3,2,1,0:T(8,128)(2,1)S(1)}, u32[]{:S(2)}, u32[]{:S(2)}) %all-to-all-start.1) | async-done | bytes 524320 | tf_op jit(solution)/shard_map/all_to_all | solution.py:116
  44.1 4.4 %all-to-all-start.2 = ((bf16[1,32,16,512]{3,2,0,1:T(8,128)(2,1)}), bf16[1,32,16,512]{3,2,0,1:T(8,128)(2,1)S(1)}, u32[]{:S(2)}, u32[]{:S(2)}) async-start(bf16[1,32,16,512]{3,2,0,1:T(8,128)(2,1)} %fusion.7), calls=%async_computation.2 | async-start | bytes 1048576 | tf_op jit(solution)/shard_map/all_to_all | solution.py:121
  48.5 1.2 fusion.5
  49.8 13.0 %all-to-all-done.2 = bf16[1,32,16,512]{3,2,0,1:T(8,128)(2,1)S(1)} async-done(((bf16[1,32,16,512]{3,2,0,1:T(8,128)(2,1)}), bf16[1,32,16,512]{3,2,0,1:T(8,128)(2,1)S(1)}, u32[]{:S(2)}, u32[]{:S(2)}) %all-to-all-start.2) | async-done | bytes 524320 | tf_op jit(solution)/shard_map/all_to_all | solution.py:121
  62.7 4.4 %all-to-all-start = ((bf16[1,32,16,512]{3,2,0,1:T(8,128)(2,1)}), bf16[1,32,16,512]{3,2,0,1:T(8,128)(2,1)S(1)}, u32[]{:S(2)}, u32[]{:S(2)}) async-start(bf16[1,32,16,512]{3,2,0,1:T(8,128)(2,1)} %fusion.5), calls=%async_computation | async-start | bytes 1048576 | tf_op jit(solution)/shard_map/all_to_all | solution.py:122
  67.1 0.7 fusion.56
  67.9 13.5 %all-to-all-done = bf16[1,32,16,512]{3,2,0,1:T(8,128)(2,1)S(1)} async-done(((bf16[1,32,16,512]{3,2,0,1:T(8,128)(2,1)}), bf16[1,32,16,512]{3,2,0,1:T(8,128)(2,1)S(1)}, u32[]{:S(2)}, u32[]{:S(2)}) %all-to-all-start) | async-done | bytes 524320 | tf_op jit(solution)/shard_map/all_to_all | solution.py:122
  82.2 18.4 %all_to_all.32 = bf16[32,1,16,512]{3,2,1,0:T(8,128)(2,1)S(1)} all-to-all(bf16[32,1,16,512]{3,2,1,0:T(8,128)(2,1)S(1)} %copy.24), channel_id=1, replica_groups=mesh['groups'=1,'tm'=32] {'tm'}, dimensions={0} | all-to-all | bytes 1048576 | tf_op jit(solution)/shard_map/all_to_all | solution.py:125
  101.3 3.0 %collective-permute-start.1 = (bf16[1,512,512]{2,1,0:T(8,128)(2,1)S(1)}, bf16[1,512,512]{2,1,0:T(8,128)(2,1)}, u32[]{:S(2)}, u32[]{:S(2)}) collective-permute-start(bf16[1,512,512]{2,1,0:T(8,128)(2,1)S(1)} %fusion.14), channel_id=1, source_target_pairs={{0,1},{1,2},{2,3},{3,4},{4,5},{5,6},{6,7},{7,8},{8,9},{9,10},{10,1... | collective-permute-start | bytes 1572872 | tf_op jit(solution)/shard_map/ppermute | solution.py:15
  104.4 3.6 %collective-permute-start = (bf16[1,512,512]{2,1,0:T(8,128)(2,1)S(1)}, bf16[1,512,512]{2,1,0:T(8,128)(2,1)}, u32[]{:S(2)}, u32[]{:S(2)}) collective-permute-start(bf16[1,512,512]{2,1,0:T(8,128)(2,1)S(1)} %fusion.14), channel_id=1, source_target_pairs={{0,2},{1,3},{2,4},{3,5},{4,6},{5,7},{6,8},{7,9},{8,10},{9,11},{10,... | collective-permute-start | bytes 1572872 | tf_op jit(solution)/shard_map/ppermute | solution.py:15
  107.9 0.6 fusion.54
  108.6 1.2 fusion.55
  111.8 1.3 collective-permute-done.1
  113.0 12.5 %collective-permute-done = bf16[1,512,512]{2,1,0:T(8,128)(2,1)} collective-permute-done((bf16[1,512,512]{2,1,0:T(8,128)(2,1)S(1)}, bf16[1,512,512]{2,1,0:T(8,128)(2,1)}, u32[]{:S(2)}, u32[]{:S(2)}) %collective-permute-start) | collective-permute-done | bytes 524320 | tf_op jit(solution)/shard_map/ppermute | solution.py:15
  125.5 1.4 %pad_maximum_fusion = bf16[3,512,512]{2,1,0:T(8,128)(2,1)S(1)} fusion(bf16[1,512,512]{2,1,0:T(8,128)(2,1)S(1)} %fusion.14, bf16[1,512,512]{2,1,0:T(8,128)(2,1)} %collective-permute-done.1, bf16[1,512,512]{2,1,0:T(8,128)(2,1)} %collective-permute-done), kind=kLoop, calls=%fused_computation.1 | loop fusion | flops 1572864 | bytes 3145728 | tf_op jit(solution)/shard_map/concatenate | solution.py:135
  126.9 1.0 fusion.28
  127.9 1.0 fusion.30
  128.9 1.5 %add_convert_fusion = bf16[512,512]{1,0:T(8,128)(2,1)S(1)} fusion(f32[1536,512]{1,0:T(8,128)S(1)} %fusion.28, f32[1536,512]{1,0:T(8,128)S(1)} %fusion.30, bf16[1536,512]{1,0:T(8,128)(2,1)S(1)} %bitcast.238, f32[]{:T(128)S(6)} %sub.31, f32[]{:T(128)S(6)} %select_n.22, f32[]{:T(128)S(6)} %convert_element_type.146, f32[]{:T(128)S(6)} %convert_element_type.145, ...), kind=kOutput, calls=%fused_computation.37 | convolution fusion | flops 277348352 | bytes 6815800 | tf_op jit(solution)/shard_map/dot_general | solution.py:66
  130.4 0.7 pad_slice_fusion
  134.6 1.2 fusion.3
  (57 shorter events, 20.2 us)
Async XLA Ops:
  0.0 100.6 %copy-start = (bf16[512,512]{1,0:T(8,128)(2,1)S(1)}, bf16[512,512]{1,0:T(8,128)(2,1)}, u32[]{:S(2)}) copy-start(bf16[512,512]{1,0:T(8,128)(2,1)} %param.12) | copy-start | bytes 1572868
  0.0 29.9 %copy-start.3 = (bf16[512,512]{1,0:T(8,128)(2,1)S(1)}, bf16[512,512]{1,0:T(8,128)(2,1)}, u32[]{:S(2)}) copy-start(bf16[512,512]{1,0:T(8,128)(2,1)} %param.10) | copy-start | bytes 1572868
  2.5 46.0 %copy-start.4 = (bf16[512,512]{1,0:T(8,128)(2,1)S(1)}, bf16[512,512]{1,0:T(8,128)(2,1)}, u32[]{:S(2)}) copy-start(bf16[512,512]{1,0:T(8,128)(2,1)} %param.11) | copy-start | bytes 1572868
  23.5 20.6 %all-to-all-start.1 = ((bf16[32,1,1,16,512]{4,3,2,1,0:T(8,128)(2,1)}), bf16[32,1,1,16,512]{4,3,2,1,0:T(8,128)(2,1)S(1)}, u32[]{:S(2)}, u32[]{:S(2)}) async-start(bf16[32,1,1,16,512]{4,3,2,1,0:T(8,128)(2,1)} %constant_dynamic-update-slice_fusion), calls=%async_computation.1 | async-start | bytes 1048576 | tf_op jit(solution)/shard_map/all_to_all | solution.py:116
  44.1 18.6 %all-to-all-start.2 = ((bf16[1,32,16,512]{3,2,0,1:T(8,128)(2,1)}), bf16[1,32,16,512]{3,2,0,1:T(8,128)(2,1)S(1)}, u32[]{:S(2)}, u32[]{:S(2)}) async-start(bf16[1,32,16,512]{3,2,0,1:T(8,128)(2,1)} %fusion.7), calls=%async_computation.2 | async-start | bytes 1048576 | tf_op jit(solution)/shard_map/all_to_all | solution.py:121
  49.7 50.9 %copy-start.1 = (bf16[1,512,512]{2,1,0:T(8,128)(2,1)S(1)}, bf16[1,512,512]{2,1,0:T(8,128)(2,1)}, u32[]{:S(2)}) copy-start(bf16[1,512,512]{2,1,0:T(8,128)(2,1)} %param.8) | copy-start | bytes 1572868
  62.7 18.6 %all-to-all-start = ((bf16[1,32,16,512]{3,2,0,1:T(8,128)(2,1)}), bf16[1,32,16,512]{3,2,0,1:T(8,128)(2,1)S(1)}, u32[]{:S(2)}, u32[]{:S(2)}) async-start(bf16[1,32,16,512]{3,2,0,1:T(8,128)(2,1)} %fusion.5), calls=%async_computation | async-start | bytes 1048576 | tf_op jit(solution)/shard_map/all_to_all | solution.py:122
  81.9 26.1 %copy-start.5 = (s32[4]{0:T(128)S(1)}, s32[4]{0:T(128)}, u32[]{:S(2)}) copy-start(s32[4]{0:T(128)} %param.15) | copy-start | bytes 52
  100.6 26.3 %copy-start.2 = (bf16[3,512,512]{2,1,0:T(8,128)(2,1)S(1)}, bf16[3,512,512]{2,1,0:T(8,128)(2,1)}, u32[]{:S(2)}) copy-start(bf16[3,512,512]{2,1,0:T(8,128)(2,1)} %param.13) | copy-start | bytes 4718596
  101.3 11.7 %collective-permute-start.1 = (bf16[1,512,512]{2,1,0:T(8,128)(2,1)S(1)}, bf16[1,512,512]{2,1,0:T(8,128)(2,1)}, u32[]{:S(2)}, u32[]{:S(2)}) collective-permute-start(bf16[1,512,512]{2,1,0:T(8,128)(2,1)S(1)} %fusion.14), channel_id=1, source_target_pairs={{0,1},{1,2},{2,3},{3,4},{4,5},{5,6},{6,7},{7,8},{8,9},{9,10},{10,1... | collective-permute-start | bytes 1572872 | tf_op jit(solution)/shard_map/ppermute | solution.py:15
  104.4 21.1 %collective-permute-start = (bf16[1,512,512]{2,1,0:T(8,128)(2,1)S(1)}, bf16[1,512,512]{2,1,0:T(8,128)(2,1)}, u32[]{:S(2)}, u32[]{:S(2)}) collective-permute-start(bf16[1,512,512]{2,1,0:T(8,128)(2,1)S(1)} %fusion.14), channel_id=1, source_target_pairs={{0,2},{1,3},{2,4},{3,5},{4,6},{5,7},{6,8},{7,9},{8,10},{9,11},{10,... | collective-permute-start | bytes 1572872 | tf_op jit(solution)/shard_map/ppermute | solution.py:15
  127.9 3.2 %slice-start = ((s8[4718592]{0:T(1024)(128)(4,1)}), s8[4194304]{0:T(1024)(128)(4,1)S(1)}, s32[]{:S(2)}) async-start(s8[4718592]{0:T(1024)(128)(4,1)} %bitcast.242), calls=%async_computation.4 | async-start | bytes 8388608
  128.8 2.2 %slice-start.1 = ((s8[4718592]{0:T(1024)(128)(4,1)}), s8[524288]{0:T(1024)(128)(4,1)S(1)}, s32[]{:S(2)}) async-start(s8[4718592]{0:T(1024)(128)(4,1)} %bitcast.242), calls=%async_computation.5 | async-start | bytes 1048576
